TPU v7x, 32 devices: a whole 2x2x4 slice. The times are simulated.
32 devices in a mesh: rep: 4 (over y, x), shard: 8 (over z, core).
Axes of the slice: x: 2, y: 2, z: 4, core: 2. Of those that a mesh axis runs over, the one named last changes fastest.
Arguments:
- tokens: bfloat16 [32, 512, 1024], P(('rep', 'shard')), may hold values from -6 to 6
- cotangent: bfloat16 [32, 512, 1024], P(('rep', 'shard')), may hold values from -6 to 6
- lengths: int32 [32], replicated, may hold values from 1 to 512, 12288 in all
- slot_sequence: int32 [32], P(('rep', 'shard')), may hold values from 0 to 31, each once
- step_count: int32 [1], replicated, may hold values from 1 to 20
- learn_rate: float32 [1], replicated, may hold values from 0.1 to 1
- attention_in: float32 [1024, 3, 1024], P('shard'), may hold values from -0.1875 to 0.1875
- attention_in_first: float32 [1024, 3, 1024], P('shard'), may hold values from -36 to 36
- attention_in_second: float32 [1024, 3, 1024], P('shard'), may hold values from 20 to 400
- attention_out: float32 [1024, 1024], P('shard'), may hold values from -1.5 to 1.5
- attention_out_first: float32 [1024, 1024], P('shard'), may hold values from -36 to 36
- attention_out_second: float32 [1024, 1024], P('shard'), may hold values from 20 to 400
- gate_up_weight: float32 [1024, 2, 2816], P('shard'), may hold values from -0.1875 to 0.1875
- gate_up_first: float32 [1024, 2, 2816], P('shard'), may hold values from -36 to 36
- gate_up_second: float32 [1024, 2, 2816], P('shard'), may hold values from 20 to 400
- down_weight: float32 [2816, 1024], P('shard'), may hold values from -0.109375 to 0.109375
- down_first: float32 [2816, 1024], P('shard'), may hold values from -36 to 36
- down_second: float32 [2816, 1024], P('shard'), may hold values from 20 to 400
Outputs:
- output: bfloat16 [32, 512, 1024], P(('rep', 'shard'))
- input_grad: float32 [32, 512, 1024], P(('rep', 'shard'))
- attention_in_grad: float32 [1024, 3, 1024], P('shard')
- attention_in_new: float32 [1024, 3, 1024], P('shard')
- attention_in_first_new: float32 [1024, 3, 1024], P('shard')
- attention_in_second_new: float32 [1024, 3, 1024], P('shard')
- attention_out_grad: float32 [1024, 1024], P('shard')
- attention_out_new: float32 [1024, 1024], P('shard')
- attention_out_first_new: float32 [1024, 1024], P('shard')
- attention_out_second_new: float32 [1024, 1024], P('shard')
- gate_up_grad: float32 [1024, 2, 2816], P('shard')
- gate_up_new: float32 [1024, 2, 2816], P('shard')
- gate_up_first_new: float32 [1024, 2, 2816], P('shard')
- gate_up_second_new: float32 [1024, 2, 2816], P('shard')
- down_grad: float32 [2816, 1024], P('shard')
- down_new: float32 [2816, 1024], P('shard')
- down_first_new: float32 [2816, 1024], P('shard')
- down_second_new: float32 [2816, 1024], P('shard')
Inputs may be any that keep to these rules, and one draw needn't show every extreme that they name: `lengths`: lengths of the sequences by number; they add up to 3 / 4 of 16384, and one is exactly 512. `slot_sequence`: A permutation of the 32 sequence numbers.
All inputs are finite; a program needn't handle non-finite values.
Results may differ from a plain program's by a relative error of at most 0.025.
The roundings to bfloat16 on the way count: a program that leaves them out, or rounds other values in their place, can miss the bound.
Values may be sent and summed in bfloat16 or wider, within the bound.
A program may use at most 256 MiB of HBM per device.

v0:
```python
import jax
import jax.numpy as jnp
from jax import lax
from jax.sharding import PartitionSpec as P

HD = 64
norm_eps = 1e-05
beta_first = 0.9
beta_second = 0.95
adam_eps = 1e-08
weight_decay = 0.1
rope_base = 10000.0
masked_score = -1e30


def layer_norm(values):
    centered = values - jnp.mean(values, axis=-1, keepdims=True)
    inverse = lax.rsqrt(jnp.mean(centered * centered, axis=-1, keepdims=True) + norm_eps)
    return (centered * inverse, inverse)


def norm_back(normed, inverse, upstream):
    mean_grad = jnp.mean(upstream, axis=-1, keepdims=True)
    mean_dot = jnp.mean(upstream * normed, axis=-1, keepdims=True)
    return inverse * (upstream - mean_grad - normed * mean_dot)


def rope_tables(position_count, head_size):
    half_size = head_size // 2
    frequency = rope_base ** (-(jnp.arange(half_size, dtype=jnp.float32) * 2.0 / head_size))
    angles = jnp.arange(position_count, dtype=jnp.float32)[:, None] * frequency[None, :]
    angles = jnp.concatenate([angles, angles], axis=1)
    return (jnp.cos(angles)[:, None, :], jnp.sin(angles)[:, None, :])


def rotate(values, cosine_table, sine_table):
    half_size = values.shape[-1] // 2
    turned = jnp.concatenate([-values[..., half_size:], values[..., :half_size]], axis=-1)
    return values * cosine_table + turned * sine_table


def masked_scores(queries, rotated_keys, length):
    position_count, head_size = (queries.shape[0], queries.shape[-1])
    scores = jnp.einsum(
        "qhd,khd->hqk", queries, rotated_keys, preferred_element_type=jnp.float32
    ) * head_size ** (-0.5)
    position = jnp.arange(position_count)
    allowed = (position[None, :] <= position[:, None]) & (position[None, :] < length)
    return jnp.where(allowed[None], scores, masked_score)


def attend_forward(pieces):
    queries, rotated_keys, values_low, length = pieces
    scores = masked_scores(queries, rotated_keys, length)
    row_max = jnp.max(scores, axis=-1, keepdims=True)
    exponent = jnp.exp(scores - row_max)
    row_sum = jnp.sum(exponent, axis=-1, keepdims=True)
    weights = (exponent / row_sum).astype(jnp.bfloat16)
    mixed_heads = jnp.einsum(
        "hqk,khd->qhd", weights, values_low, preferred_element_type=jnp.float32
    )
    return (mixed_heads, row_max + jnp.log(row_sum))


def attend_backward(pieces):
    queries, rotated_keys, values_low, length, log_total, mixed_grad = pieces
    head_size = queries.shape[-1]
    scores = masked_scores(queries, rotated_keys, length)
    probability = jnp.exp(scores - log_total)
    value_grad = jnp.einsum(
        "hqk,qhd->khd",
        probability.astype(jnp.bfloat16),
        mixed_grad,
        preferred_element_type=jnp.float32,
    )
    probability_grad = jnp.einsum(
        "qhd,khd->hqk", mixed_grad, values_low, preferred_element_type=jnp.float32
    )
    inner_dot = jnp.sum(probability * probability_grad, axis=-1, keepdims=True)
    score_grad = (probability * (probability_grad - inner_dot) * head_size ** (-0.5)).astype(
        jnp.bfloat16
    )
    query_grad = jnp.einsum(
        "hqk,khd->qhd", score_grad, rotated_keys, preferred_element_type=jnp.float32
    )
    key_grad = jnp.einsum("hqk,qhd->khd", score_grad, queries, preferred_element_type=jnp.float32)
    return (query_grad, key_grad, value_grad)


def adam_update(weight, first, second, gradient, step_count, learn_rate):
    steps_taken = step_count[0].astype(jnp.float32)
    first_new = beta_first * first + (1.0 - beta_first) * gradient
    second_new = beta_second * second + (1.0 - beta_second) * gradient * gradient
    first_hat = first_new / (1.0 - beta_first**steps_taken)
    second_hat = second_new / (1.0 - beta_second**steps_taken)
    weight_new = weight - learn_rate[0] * (
        first_hat / (jnp.sqrt(second_hat) + adam_eps) + weight_decay * weight
    )
    return (gradient, weight_new, first_new, second_new)


def gather_full(local, rep_count, rep_index):
    rows = local.shape[0]
    flat = local.reshape(rows, -1)
    width = flat.shape[1] // rep_count
    piece = lax.dynamic_slice_in_dim(flat, rep_index * width, width, axis=1)
    column = lax.all_gather(piece, "shard", axis=0, tiled=True)
    return lax.all_gather(column, "rep", axis=0, tiled=False)


def reduce_full(partial):
    part = lax.psum_scatter(partial, "rep", scatter_dimension=0, tiled=False)
    part = lax.psum_scatter(part, "shard", scatter_dimension=0, tiled=True)
    pieces = lax.all_gather(part, "rep", axis=0, tiled=False)
    rows = pieces.shape[1]
    return jnp.transpose(pieces, (1, 0, 2)).reshape(rows, -1).astype(jnp.float32)


def shards(
    tokens,
    cotangent,
    lengths,
    slot_sequence,
    step_count,
    learn_rate,
    attention_in,
    attention_in_first,
    attention_in_second,
    attention_out,
    attention_out_first,
    attention_out_second,
    gate_up_weight,
    gate_up_first,
    gate_up_second,
    down_weight,
    down_first,
    down_second,
):
    slot_count, position_count, feature_count = tokens.shape
    row_total = slot_count * position_count
    head_count = feature_count // HD
    shaped = (slot_count, position_count, head_count, HD)
    inputs = tokens.astype(jnp.float32).reshape(row_total, feature_count)
    matches = jnp.arange(lengths.shape[0])[None, :] == slot_sequence[:, None]
    slot_length = jnp.sum(jnp.where(matches, lengths[None, :], 0), axis=1)
    alive_rows = (
        (jnp.arange(position_count)[None, :] < slot_length[:, None])
        .astype(jnp.float32)
        .reshape(row_total, 1)
    )
    cosine_table, sine_table = rope_tables(position_count, HD)
    in_local = attention_in.astype(jnp.bfloat16)
    out_local = attention_out.astype(jnp.bfloat16)
    gate_up_local = gate_up_weight.astype(jnp.bfloat16)
    down_local = down_weight.astype(jnp.bfloat16)
    rep_count = lax.axis_size("rep")
    rep_index = lax.axis_index("rep")
    in_full = gather_full(in_local, rep_count, rep_index)
    out_full = gather_full(out_local, rep_count, rep_index)
    gate_up_full = gather_full(gate_up_local, rep_count, rep_index)
    down_full = gather_full(down_local, rep_count, rep_index)
    normed_one, inverse_one = layer_norm(inputs)
    first_input = normed_one.astype(jnp.bfloat16)
    projected = jnp.einsum(
        "rd,qde->rqe", first_input, in_full, preferred_element_type=jnp.float32
    ).reshape(row_total, 3, feature_count)
    queries = rotate(projected[:, 0].reshape(shaped), cosine_table, sine_table).astype(jnp.bfloat16)
    rotated_keys = rotate(projected[:, 1].reshape(shaped), cosine_table, sine_table).astype(
        jnp.bfloat16
    )
    values_low = projected[:, 2].reshape(shaped).astype(jnp.bfloat16)
    mixed_heads, log_total = lax.map(
        attend_forward, (queries, rotated_keys, values_low, slot_length)
    )
    mixed_low = mixed_heads.reshape(row_total, feature_count).astype(jnp.bfloat16)
    residual = inputs + jnp.einsum(
        "rd,qde->rqe", mixed_low, out_full, preferred_element_type=jnp.float32
    ).reshape(row_total, feature_count)
    normed_two, inverse_two = layer_norm(residual)
    second_input = normed_two.astype(jnp.bfloat16)
    gate_up = jnp.einsum(
        "rd,qdf->rqf", second_input, gate_up_full, preferred_element_type=jnp.float32
    ).reshape(row_total, 2, -1)
    gate_value = gate_up[:, 0]
    up_value = gate_up[:, 1]
    sigmoid_gate = jax.nn.sigmoid(gate_value)
    hidden_low = (gate_value * sigmoid_gate * up_value).astype(jnp.bfloat16)
    result = residual + jnp.einsum(
        "rf,qfe->rqe", hidden_low, down_full, preferred_element_type=jnp.float32
    ).reshape(row_total, feature_count)
    output = (result * alive_rows).astype(jnp.bfloat16).reshape(tokens.shape)
    output_grad = cotangent.astype(jnp.float32).reshape(row_total, feature_count) * alive_rows
    result_grad_low = output_grad.astype(jnp.bfloat16)
    hidden_grad = jnp.einsum(
        "rqe,qfe->rf",
        result_grad_low.reshape(row_total, rep_count, -1),
        down_full,
        preferred_element_type=jnp.float32,
    )
    gate_grad = hidden_grad * up_value * sigmoid_gate * (1.0 + gate_value * (1.0 - sigmoid_gate))
    up_grad = hidden_grad * gate_value * sigmoid_gate
    gate_up_grad_low = (
        jnp.concatenate([gate_grad, up_grad], axis=1)
        .astype(jnp.bfloat16)
        .reshape(row_total, rep_count, -1)
    )
    second_input_grad = jnp.einsum(
        "rqf,qdf->rd", gate_up_grad_low, gate_up_full, preferred_element_type=jnp.float32
    )
    residual_grad = output_grad + norm_back(normed_two, inverse_two, second_input_grad)
    down_part = reduce_full(
        jnp.einsum(
            "rc,rqe->qce",
            hidden_low,
            result_grad_low.reshape(row_total, rep_count, -1),
            preferred_element_type=jnp.float32,
        ).astype(jnp.bfloat16)
    )
    gate_up_part = reduce_full(
        jnp.einsum(
            "rc,rqf->qcf", second_input, gate_up_grad_low, preferred_element_type=jnp.float32
        ).astype(jnp.bfloat16)
    ).reshape(gate_up_weight.shape)
    branch_grad = residual_grad.astype(jnp.bfloat16)
    mixed_grad = (
        jnp.einsum(
            "rqe,qde->rd",
            branch_grad.reshape(row_total, rep_count, -1),
            out_full,
            preferred_element_type=jnp.float32,
        )
        .astype(jnp.bfloat16)
        .reshape(shaped)
    )
    query_grad, key_grad, value_grad = lax.map(
        attend_backward, (queries, rotated_keys, values_low, slot_length, log_total, mixed_grad)
    )
    query_back = rotate(query_grad, cosine_table, -sine_table).reshape(row_total, feature_count)
    key_back = rotate(key_grad, cosine_table, -sine_table).reshape(row_total, feature_count)
    projected_grad = (
        jnp.concatenate(
            [query_back, key_back, value_grad.reshape(row_total, feature_count)], axis=1
        )
        .astype(jnp.bfloat16)
        .reshape(row_total, rep_count, -1)
    )
    first_input_grad = jnp.einsum(
        "rqe,qde->rd", projected_grad, in_full, preferred_element_type=jnp.float32
    )
    input_grad = (residual_grad + norm_back(normed_one, inverse_one, first_input_grad)).reshape(
        tokens.shape
    )
    in_part = reduce_full(
        jnp.einsum(
            "rc,rqe->qce", first_input, projected_grad, preferred_element_type=jnp.float32
        ).astype(jnp.bfloat16)
    ).reshape(attention_in.shape)
    out_part = reduce_full(
        jnp.einsum(
            "rc,rqe->qce",
            mixed_low,
            branch_grad.reshape(row_total, rep_count, -1),
            preferred_element_type=jnp.float32,
        ).astype(jnp.bfloat16)
    )
    in_grad, in_new, in_first, in_second = adam_update(
        attention_in, attention_in_first, attention_in_second, in_part, step_count, learn_rate
    )
    out_grad, out_new, out_first, out_second = adam_update(
        attention_out, attention_out_first, attention_out_second, out_part, step_count, learn_rate
    )
    gu_grad, gu_new, gu_first, gu_second = adam_update(
        gate_up_weight, gate_up_first, gate_up_second, gate_up_part, step_count, learn_rate
    )
    dn_grad, dn_new, dn_first, dn_second = adam_update(
        down_weight, down_first, down_second, down_part, step_count, learn_rate
    )
    return (
        output,
        input_grad,
        in_grad,
        in_new,
        in_first,
        in_second,
        out_grad,
        out_new,
        out_first,
        out_second,
        gu_grad,
        gu_new,
        gu_first,
        gu_second,
        dn_grad,
        dn_new,
        dn_first,
        dn_second,
    )


def solution(mesh):
    return jax.shard_map(
        shards,
        mesh=mesh,
        in_specs=(
            P(("rep", "shard"), None, None),
            P(("rep", "shard"), None, None),
            P(),
            P(("rep", "shard")),
            P(),
            P(),
            P("shard", None, None),
            P("shard", None, None),
            P("shard", None, None),
            P("shard", None),
            P("shard", None),
            P("shard", None),
            P("shard", None, None),
            P("shard", None, None),
            P("shard", None, None),
            P("shard", None),
            P("shard", None),
            P("shard", None),
        ),
        out_specs=(
            P(("rep", "shard"), None, None),
            P(("rep", "shard"), None, None),
            P("shard", None, None),
            P("shard", None, None),
            P("shard", None, None),
            P("shard", None, None),
            P("shard", None),
            P("shard", None),
            P("shard", None),
            P("shard", None),
            P("shard", None, None),
            P("shard", None, None),
            P("shard", None, None),
            P("shard", None, None),
            P("shard", None),
            P("shard", None),
            P("shard", None),
            P("shard", None),
        ),
        check_vma=False,
    )
```

profile of v0, /device:TPU:0, one launch (start us, length us, event | category | flops | bytes accessed | tf_op | source)
XLA Modules:
  0.0 931.0 jit_solution(1859404770817627660)
XLA Ops:
  16.7 19.5 %all_gather.63 = bf16[1024,256]{1,0:T(8,128)(2,1)} all-gather(bf16[128,256]{1,0:T(8,128)(2,1)S(1)} %dynamic-slice_convert_fusion.1), channel_id=1, replica_groups=mesh['rep'=4,'shard'=8] {'shard'}, dimensions={0}, use_global_device_ids=true | all-gather | bytes 589824 | tf_op jit(solution)/shard_map/all_gather | solution.py:107
  36.2 7.5 all-gather.17.cloned.1.call-done
  43.8 37.6 %all-gather.19.cloned.1.call-done = bf16[1024,1408]{1,0:T(8,128)(2,1)} async-done(((bf16[128,1408]{1,0:T(8,128)(2,1)}), bf16[1024,1408]{1,0:T(8,128)(2,1)}) %all-gather.19.cloned.1.call-update) | async-done | bytes 2883600 | tf_op jit(solution)/shard_map/all_gather | solution.py:107
  88.0 18.9 %all-gather.21.cloned.1.call-done = bf16[2816,256]{1,0:T(8,128)(2,1)} async-done(((bf16[352,256]{1,0:T(8,128)(2,1)}), bf16[2816,256]{1,0:T(8,128)(2,1)}) %all-gather.21.cloned.1.call-update) | async-done | bytes 1441808 | tf_op jit(solution)/shard_map/all_gather | solution.py:107
  107.4 36.0 %all-gather.25.cloned.1.call-done = bf16[4096,256]{1,0:T(8,128)(2,1)} async-done(((bf16[1024,256]{1,0:T(8,128)(2,1)}), bf16[4096,256]{1,0:T(8,128)(2,1)}) %all-gather.25.cloned.1.call-update) | async-done | bytes 2097168 | tf_op jit(solution)/shard_map/all_gather | solution.py:108
  147.4 67.9 %all-gather.23.cloned.1.call-done = bf16[4096,768]{0,1:T(8,128)(2,1)} async-done(((bf16[1024,768]{0,1:T(8,128)(2,1)}), bf16[4096,768]{0,1:T(8,128)(2,1)}) %all-gather.23.cloned.1.call-update) | async-done | bytes 6291472 | tf_op jit(solution)/shard_map/all_gather | solution.py:108
  215.3 8.6 copy.182
  224.0 9.0 copy.183
  263.5 10.3 %fusion.4 = f32[16,512]{1,0:T(8,128)S(1)} fusion(f32[16,512,512]{1,2,0:T(8,128)} %get-tuple-element.181, f32[16,512]{1,0:T(8,128)S(1)} %get-tuple-element.180), kind=kLoop, calls=%fused_computation.8 | loop fusion | flops 8380416 | bytes 16842752 | tf_op jit(solution)/shard_map/while/body/eval_jaxpr/reduce_sum | solution.py:57
  273.8 7.9 fusion.60
  284.8 46.0 %all-gather.27.cloned.1.call-done = bf16[4096,1408]{1,0:T(8,128)(2,1)} async-done(((bf16[1024,1408]{1,0:T(8,128)(2,1)}), bf16[4096,1408]{1,0:T(8,128)(2,1)}) %all-gather.27.cloned.1.call-update) | async-done | bytes 11534352 | tf_op jit(solution)/shard_map/all_gather | solution.py:108
  330.9 12.5 %fusion.79 = f32[512,4,1408]{0,2,1:T(8,128)} fusion(bf16[4,1024,1408]{2,1,0:T(8,128)(2,1)} %bitcast.296, f32[512,1024]{1,0:T(8,128)} %copy-done.7, f32[512]{0:T(512)S(1)} %add_rsqrt_fusion, f32[512]{0:T(512)S(1)} %broadcast_multiply_fusion.4), kind=kOutput, calls=%fused_computation.134 | convolution fusion | flops 5907152896 | bytes 25169920 | tf_op jit(solution)/shard_map/rd,qdf->rqf/dot_general | solution.py:181
  343.4 9.9 %fusion.97 = (f32[512,1,2816]{0,2,1:T(8,128)}, f32[512,1,2816]{0,2,1:T(8,128)}) fusion(f32[512,2,2816]{0,2,1:T(8,128)} %bitcast.256), kind=kLoop, calls=%fused_computation.157 | loop fusion | bytes 23068672 | tf_op jit(solution)/shard_map/slice | solution.py:184
  365.9 32.7 %all-gather.29.cloned.1.call-done = bf16[11264,256]{1,0:T(8,128)(2,1)} async-done(((bf16[2816,256]{1,0:T(8,128)(2,1)}), bf16[11264,256]{1,0:T(8,128)(2,1)}) %all-gather.29.cloned.1.call-update) | async-done | bytes 5767184 | tf_op jit(solution)/shard_map/all_gather | solution.py:108
  398.5 11.1 %fusion.25 = (bf16[512,2816]{1,0:T(8,128)(2,1)S(1)}, bf16[512,2816]{1,0:T(8,128)(2,1)S(1)}) fusion(f32[512,1,2816]{2,0,1:T(8,128)} %copy.240, f32[512,1,2816]{2,0,1:T(8,128)} %copy.241, bf16[4,2816,256]{2,1,0:T(8,128)(2,1)} %bitcast.263, f32[512,4,256]{2,1,0:T(4,128)} %reshape.396, f32[512]{0:T(512)S(1)} %fusion.87), kind=kOutput, calls=%fused_computation.30 | convolution fusion | flops 2972581888 | bytes 25167872 | tf_op jit(solution)/shard_map/rqe,qfe->rf/dot_general | solution.py:194
  414.0 11.1 %bitcast_reduce_fusion.1 = (f32[512]{0:T(512)S(1)}, f32[512]{0:T(512)S(1)}, f32[512,1024,1]{1,0,2:T(8,128)S(1)}) fusion(f32[512]{0:T(512)S(1)} %add_rsqrt_fusion, f32[512,1024]{1,0:T(8,128)S(1)} %copy-done.8, f32[512]{0:T(512)S(1)} %broadcast_multiply_fusion.4, bf16[512,4,1408]{2,0,1:T(8,128)(2,1)} %bitcast_dynamic-update-slice_fusion, ...), kind=kOutput, calls=%fused_computation.81 | convolution fusion | flops 5908200448 | bytes 21504000 | tf_op jit(solution)/shard_map/rqf,qdf->rd/dot_general | solution.py:207
  432.8 12.2 %fusion.6 = bf16[4,1024,1408]{1,2,0:T(8,128)(2,1)} fusion(bf16[512,4,1408]{2,0,1:T(8,128)(2,1)} %bitcast_dynamic-update-slice_fusion, f32[512,1024]{1,0:T(8,128)} %copy-done.7, f32[512]{0:T(512)S(1)} %add_rsqrt_fusion, f32[512]{0:T(512)S(1)} %broadcast_multiply_fusion.4), kind=kOutput, calls=%fused_computation.11 | convolution fusion | flops 5912920064 | bytes 19402752 | tf_op jit(solution)/shard_map/rc,rqf->qcf/dot_general | solution.py:220
  465.8 8.2 fusion.101
  474.0 26.2 %fusion.16 = f32[16,64,512]{2,1,0:T(8,128)} fusion(bf16[512,16,64]{0,2,1:T(8,128)(2,1)} %copy-done.22, f32[16,512,512]{1,2,0:T(8,128)} %fusion.101, f32[16,512,512]{1,2,0:T(8,128)} %get-tuple-element.181, f32[16,512]{1,0:T(8,128)S(1)} %log_add_fusion), kind=kOutput, calls=%fused_computation.19 | convolution fusion | flops 566239744 | bytes 36732928 | tf_op jit(solution)/shard_map/while/body/eval_jaxpr/hqk,khd->qhd/dot_general | solution.py:83
  503.8 26.1 %fusion.13 = f32[16,64,512]{2,1,0:T(8,128)} fusion(bf16[512,16,64]{0,2,1:T(8,128)(2,1)S(1)} %copy-done.21, f32[16,512,512]{1,2,0:T(8,128)} %fusion.101, f32[16,512,512]{1,2,0:T(8,128)} %get-tuple-element.181, f32[16,512]{1,0:T(8,128)S(1)} %log_add_fusion), kind=kOutput, calls=%fused_computation.18 | convolution fusion | flops 566239744 | bytes 36732928 | tf_op jit(solution)/shard_map/while/body/eval_jaxpr/hqk,qhd->khd/dot_general | solution.py:86
  535.6 8.6 fusion.7
  554.3 29.4 %reduce-scatter.37.cloned.1.call-done = bf16[1,1024,1408]{1,2,0:T(8,128)(2,1)} async-done(((bf16[4,1024,1408]{1,2,0:T(8,128)(2,1)}), bf16[1,1024,1408]{1,2,0:T(8,128)(2,1)}) %reduce-scatter.37.cloned.1.call-update) | async-done | bytes 2883600
  588.3 64.4 %reduce-scatter.39.cloned.1.call-done = bf16[1,2816,256]{1,2,0:T(8,128)(2,1)} async-done(((bf16[4,2816,256]{1,2,0:T(8,128)(2,1)}), bf16[1,2816,256]{1,2,0:T(8,128)(2,1)}) %reduce-scatter.39.cloned.1.call-update) | async-done | bytes 1441808
  655.2 70.9 %reduce-scatter.33.cloned.1.call-done = bf16[1,1024,768]{1,2,0:T(8,128)(2,1)} async-done(((bf16[4,1024,768]{1,2,0:T(8,128)(2,1)}), bf16[1,1024,768]{1,2,0:T(8,128)(2,1)}) %reduce-scatter.33.cloned.1.call-update) | async-done | bytes 1572880
  736.2 8.3 copy.194
  760.9 9.4 %all-gather.5 = bf16[512,256]{0,1:T(8,128)(2,1)S(1)} all-gather(bf16[128,256]{0,1:T(8,128)(2,1)S(1)} %copy.235), channel_id=7, replica_groups=mesh['rep'=4,'shard'=8] {'rep'}, dimensions={0}, use_global_device_ids=true | all-gather | bytes 327680 | tf_op jit(solution)/shard_map/all_gather | solution.py:114
  770.8 28.9 %reduce-scatter.29.cloned.1.call-done = bf16[128,1408]{1,0:T(8,128)(2,1)} async-done(((bf16[1024,1408]{1,0:T(8,128)(2,1)}), bf16[128,1408]{1,0:T(8,128)(2,1)}) %reduce-scatter.29.cloned.1.call-update) | async-done | bytes 360464
  803.1 32.4 %reduce-scatter.31.cloned.1.call-done = bf16[352,256]{1,0:T(8,128)(2,1)} async-done(((bf16[2816,256]{1,0:T(8,128)(2,1)}), bf16[352,256]{1,0:T(8,128)(2,1)}) %reduce-scatter.31.cloned.1.call-update) | async-done | bytes 180240 | tf_op jit(solution)/shard_map/reduce_scatter | solution.py:113
  835.5 11.4 %all-gather.7 = bf16[1408,256]{1,0:T(8,128)(2,1)S(1)} all-gather(bf16[352,256]{1,0:T(8,128)(2,1)} %reduce-scatter.31.cloned.1.call-done), channel_id=9, replica_groups=mesh['rep'=4,'shard'=8] {'rep'}, dimensions={0}, use_global_device_ids=true | all-gather | bytes 901120 | tf_op jit(solution)/shard_map/all_gather | solution.py:114
  852.6 18.0 %reduce-scatter.25.cloned.1.call-done = bf16[128,768]{1,0:T(8,128)(2,1)} async-done(((bf16[1024,768]{1,0:T(8,128)(2,1)}), bf16[128,768]{1,0:T(8,128)(2,1)}) %reduce-scatter.25.cloned.1.call-update) | async-done | bytes 196624 | tf_op jit(solution)/shard_map/reduce_scatter | solution.py:113
  870.7 15.6 %all-gather.4 = bf16[512,768]{1,0:T(8,128)(2,1)S(1)} all-gather(bf16[128,768]{1,0:T(8,128)(2,1)} %reduce-scatter.25.cloned.1.call-done), channel_id=6, replica_groups=mesh['rep'=4,'shard'=8] {'rep'}, dimensions={0}, use_global_device_ids=true | all-gather | bytes 983040 | tf_op jit(solution)/shard_map/all_gather | solution.py:114
  912.1 12.2 %multiply_subtract_fusion = (f32[128,2,2816]{2,1,0:T(2,128)}, f32[128,2,2816]{2,1,0:T(2,128)}, f32[128,2,2816]{2,1,0:T(2,128)}) fusion(f32[128,2,2816]{2,1,0:T(2,128)S(1)} %copy-done.3, f32[]{:T(128)} %bitcast.61, f32[]{:T(128)} %bitcast.60, f32[]{:T(128)} %bitcast.246, f32[128,2,2816]{2,1,0:T(2,128)} %reshape.404, f32[128,2,2816]{2,1,0:T(2,128)} %param.32, ...), kind=kLoop, calls=%fused_computation.45 | loop fusion | flops 10813440 | bytes 20185100 | tf_op jit(solution)/shard_map/sub | solution.py:96
  (210 shorter events, 185.2 us)
Async XLA Ops:
  7.2 36.6 %all-gather.17.cloned.1.call-start = ((), (), s32[]{:S(2)}) async-start(), calls=%async_computation.8 | async-start | bytes 1769472 | tf_op jit(solution)/shard_map/all_gather | solution.py:107
  10.1 71.3 %all-gather.19.cloned.1.call-start = ((), (), s32[]{:S(2)}) async-start(), calls=%async_computation.9 | async-start | bytes 3244032 | tf_op jit(solution)/shard_map/all_gather | solution.py:107
  14.0 92.9 %all-gather.21.cloned.1.call-start = ((), (), s32[]{:S(2)}) async-start(), calls=%async_computation.10 | async-start | bytes 1622016 | tf_op jit(solution)/shard_map/all_gather | solution.py:107
  15.7 127.7 %all-gather.25.cloned.1.call-start = ((), (), s32[]{:S(2)}) async-start(), calls=%async_computation.12 | async-start | bytes 2621440 | tf_op jit(solution)/shard_map/all_gather | solution.py:108
  36.2 179.1 %all-gather.23.cloned.1.call-start = ((), (), s32[]{:S(2)}) async-start(), calls=%async_computation.11 | async-start | bytes 7864320 | tf_op jit(solution)/shard_map/all_gather | solution.py:108
  43.7 38.5 %copy-start.4 = (bf16[1,512,1024]{2,1,0:T(8,128)(2,1)S(1)}, bf16[1,512,1024]{2,1,0:T(8,128)(2,1)}, u32[]{:S(2)}) copy-start(bf16[1,512,1024]{2,1,0:T(8,128)(2,1)} %param.19) | copy-start | bytes 3145732
  43.8 287.1 %all-gather.27.cloned.1.call-start = ((), (), s32[]{:S(2)}) async-start(), calls=%async_computation.13 | async-start | bytes 14417920 | tf_op jit(solution)/shard_map/all_gather | solution.py:108
  81.5 317.1 %all-gather.29.cloned.1.call-start = ((), (), s32[]{:S(2)}) async-start(), calls=%async_computation.14 | async-start | bytes 7208960 | tf_op jit(solution)/shard_map/all_gather | solution.py:108
  87.4 145.6 %copy-start.39 = (f32[512]{0:T(512)}, f32[512]{0:T(512)S(1)}, u32[]{:S(2)}) copy-start(f32[512]{0:T(512)S(1)} %broadcast_multiply_fusion.5) | copy-start | bytes 6148
  87.8 145.2 %copy-start.41 = (f32[512]{0:T(512)}, f32[512]{0:T(512)S(1)}, u32[]{:S(2)}) copy-start(f32[512]{0:T(512)S(1)} %add_rsqrt_fusion.1) | copy-start | bytes 6148
  106.9 445.2 %reduce-scatter.35.cloned.1.call-start = ((), (), s32[]{:S(2)}) async-start(), calls=%async_computation.21 | async-start | bytes 2621440
  256.0 7.5 copy-start.20
  256.0 7.5 copy-start.22
  263.5 10.3 %copy-start.37 = (f32[16,512]{1,0:T(8,128)}, f32[16,512]{1,0:T(8,128)S(1)}, u32[]{:S(2)}) copy-start(f32[16,512]{1,0:T(8,128)S(1)} %get-tuple-element.180) | copy-start | bytes 98308
  263.5 10.3 %copy-start.18 = (bf16[512,1,1024]{0,2,1:T(8,128)(2,1)S(1)}, bf16[512,1,1024]{0,2,1:T(8,128)(2,1)}, u32[]{:S(2)}) copy-start(bf16[512,1,1024]{0,2,1:T(8,128)(2,1)} %copy.184) | copy-start | bytes 3145732
  273.8 7.9 copy-start.6
  273.8 7.9 copy-start.26
  432.7 150.9 %reduce-scatter.37.cloned.1.call-start = ((), (), s32[]{:S(2)}) async-start(), calls=%async_computation.22 | async-start | bytes 14417920
  445.0 207.7 %reduce-scatter.39.cloned.1.call-start = ((), (), s32[]{:S(2)}) async-start(), calls=%async_computation.23 | async-start | bytes 7208960
  458.7 267.4 %reduce-scatter.33.cloned.1.call-start = ((), (), s32[]{:S(2)}) async-start(), calls=%async_computation.20 | async-start | bytes 7864320
  503.7 28.1 %copy-start.33 = (f32[512,64]{0,1:T(8,128)S(1)}, f32[512,64]{0,1:T(8,128)}, u32[]{:S(2)}) copy-start(f32[512,64]{0,1:T(8,128)} %get-tuple-element.177) | copy-start | bytes 393220
  551.9 208.0 %reduce-scatter.27.cloned.1.call-start = ((), (), s32[]{:S(2)}) async-start(), calls=%async_computation.17 | async-start | bytes 589824
  554.2 245.5 %reduce-scatter.29.cloned.1.call-start = ((), (), s32[]{:S(2)}) async-start(), calls=%async_computation.18 | async-start | bytes 3244032
  588.2 247.3 %reduce-scatter.31.cloned.1.call-start = ((), (), s32[]{:S(2)}) async-start(), calls=%async_computation.19 | async-start | bytes 1622016 | tf_op jit(solution)/shard_map/reduce_scatter | solution.py:113
  655.2 215.5 %reduce-scatter.25.cloned.1.call-start = ((), (), s32[]{:S(2)}) async-start(), calls=%async_computation.16 | async-start | bytes 1769472 | tf_op jit(solution)/shard_map/reduce_scatter | solution.py:113
  728.7 172.1 %all-gather.31.cloned.1.call-start = ((), (), s32[]{:S(2)}) async-start(), calls=%async_computation.15 | async-start | bytes 1802240 | tf_op jit(solution)/shard_map/all_gather | solution.py:114
  744.5 7.3 copy-start.12
  744.5 9.3 copy-start.15
  760.8 40.9 %copy-start.32 = (f32[128,1024]{1,0:T(8,128)S(1)}, f32[128,1024]{1,0:T(8,128)}, u32[]{:S(2)}) copy-start(f32[128,1024]{1,0:T(8,128)} %param.27) | copy-start | bytes 1572868
  760.8 40.9 %copy-start.35 = (f32[128,1024]{1,0:T(8,128)S(1)}, f32[128,1024]{1,0:T(8,128)}, u32[]{:S(2)}) copy-start(f32[128,1024]{1,0:T(8,128)} %param.29) | copy-start | bytes 1572868
  760.9 40.9 %copy-start.36 = (f32[128,1024]{1,0:T(8,128)S(1)}, f32[128,1024]{1,0:T(8,128)}, u32[]{:S(2)}) copy-start(f32[128,1024]{1,0:T(8,128)} %param.28) | copy-start | bytes 1572868
  770.8 32.3 %copy-start.27 = (f32[16,8,4,256]{3,1,2,0:T(8,128)}, f32[16,8,4,256]{3,1,2,0:T(8,128)S(1)}, u32[]{:S(2)}) copy-start(f32[16,8,4,256]{3,1,2,0:T(8,128)S(1)} %copy.247) | copy-start | bytes 1572868
  (29 other events, 69.7 us)
Sparse Core Ops, SparseCore 0:
  10.3 33.4 all-gather.16
  46.0 35.4 all-gather.18
  83.6 23.2 all-gather.20
  108.6 34.8 all-gather.24
  145.1 70.1 all-gather.22
  217.0 113.7 all-gather.26
  332.7 65.7 all-gather.28
  432.9 35.1 reduce-scatter.34
  471.5 112.1 reduce-scatter.36
  586.8 65.8 reduce-scatter.38
  655.9 70.1 reduce-scatter.32
  728.9 30.9 reduce-scatter.26
  762.8 36.9 reduce-scatter.28
  802.5 32.9 reduce-scatter.30
  838.3 32.3 reduce-scatter.24
  872.9 27.8 all-gather.30
where the time goes:
time: 937 us; the launch traced here: 931 us
  waiting for transfers between devices  493 us (53%)
  matrix products  169 us (18%)
  local copies, waits for them, and re-layouts  134 us (14%)
  other arithmetic  61.3 us (7%)
  blocking collectives  55.9 us (6%)
  between operations  17 us (2%)
    unnamed x22, waiting for transfers between devices  195 us
    all_gather x4, waiting for transfers between devices, gather_full(): return lax.all_gather(column, 'rep', axis=0, tiled=False)  183 us
    all_gather x3, waiting for transfers between devices, gather_full(): column = lax.all_gather(piece, 'shard', axis=0, tiled=True)  64 us
    unnamed x108, local copies, waits for them, and re-layouts  59.1 us
    reduce_scatter x2, waiting for transfers between devices, reduce_full(): part = lax.psum_scatter(part, 'shard', scatter_dimension=0, tiled=True)  50.5 us
    all_gather x3, blocking collectives, reduce_full(): pieces = lax.all_gather(part, 'rep', axis=0, tiled=False)  36.4 us
    dot_general x1, matrix products, attend_backward(): jnp.einsum('hqk,khd->qhd', score_grad, rotated_keys, preferred_element_ty...  26.2 us
    dot_general x1, matrix products, attend_backward(): jnp.einsum('hqk,qhd->khd', score_grad, queries, preferred_element_type=jn...  26.1 us
  transfers between devices with their start and end apart: 16, of which 15 were waited for; matrix products, arithmetic and copies ran while one was open for 31% of the time, Pallas kernels for 0%

commit v1 on v0

--- a/solution.py
+++ b/solution.py
@@ -11,6 +11,12 @@
 weight_decay = 0.1
 rope_base = 10000.0
 masked_score = -1e30
+
+
+def laid_out(blocks, dim):
+    shape = list(blocks.shape[1:])
+    shape[dim] *= blocks.shape[0]
+    return jnp.moveaxis(blocks, 0, dim).reshape(shape)
 
 
 def layer_norm(values):
@@ -104,7 +110,19 @@
     flat = local.reshape(rows, -1)
     width = flat.shape[1] // rep_count
     piece = lax.dynamic_slice_in_dim(flat, rep_index * width, width, axis=1)
-    column = lax.all_gather(piece, "shard", axis=0, tiled=True)
+    devices = lax.axis_size("shard")
+    pairs = [(i, (i + 1) % devices) for i in range(devices)]
+    back = [(b, a) for a, b in pairs]
+    lower, upper = ([], [])
+    for turn in range(devices - 1):
+        if turn % 2 == 0:
+            lower.append(lax.ppermute(lower[-1] if lower else piece, "shard", pairs))
+        else:
+            upper.append(lax.ppermute(upper[-1] if upper else piece, "shard", back))
+    blocks = jnp.stack([*lower[::-1], piece, *upper])
+    shift = lax.axis_index("shard") - len(lower)
+    blocks = blocks[(jnp.arange(devices) - shift) % devices]
+    column = laid_out(blocks, 0)
     return lax.all_gather(column, "rep", axis=0, tiled=False)
 
 

time: 937 us -> 869 us (0.927)
  waiting for transfers between devices: 493 us -> 391 us
  starting transfers between devices: 1.29 us -> 45.7 us
  blocking collectives: 55.9 us -> 35.7 us
    all_gather x4, waiting for transfers between devices: 183 us -> 76.6 us  [gather_full(): return lax.all_gather(column, 'rep', axis=0, tiled=False)]
    ppermute x0 -> x28, waiting for transfers between devices: none -> 67.1 us  [the longest x16 63.7 us: gather_full(): lower.append(lax.ppermute(lower[-1] if lower else piece, 'shard', pairs))]
    all_gather x3 -> x0, waiting for transfers between devices: 64 us -> none  [gather_full(): column = lax.all_gather(piece, 'shard', axis=0, tiled=True)]
    ppermute x0 -> x28, starting transfers between devices: none -> 44.5 us  [the longest x12 43.7 us: gather_full(): upper.append(lax.ppermute(upper[-1] if upper else piece, 'shard', back))]
    all_gather x1 -> x0, blocking collectives: 19.5 us -> none  [gather_full(): column = lax.all_gather(piece, 'shard', axis=0, tiled=True)]
    dot_general x2 -> x0, local copies, waits for them, and re-layouts: 12.3 us -> none  [the longest x1 8.32 us: shards(): jnp.einsum('rf,qfe->rqe', hidden_low, down_full, preferred_element_type=j...]
    gather x0 -> x5, local copies, waits for them, and re-layouts: none -> 11.5 us  [gather_full(): blocks = blocks[(jnp.arange(devices) - shift) % devices]]
    unnamed x108 -> x144, local copies, waits for them, and re-layouts: 59.1 us -> 66.8 us
  transfers between devices with their start and end apart: 16 -> 41, of which waited for: 15 -> 31; matrix products, arithmetic and copies ran while one was open for 31% -> 35% of each run, Pallas kernels for 0% -> 0%
where the time goes in v1:
time: 869 us; the launch traced here: 861 us
  waiting for transfers between devices  391 us (45%)
  matrix products  169 us (19%)
  local copies, waits for them, and re-layouts  143 us (16%)
  other arithmetic  59.4 us (7%)
  starting transfers between devices  45.7 us (5%)
  blocking collectives  35.7 us (4%)
  between operations  17.1 us (2%)
    unnamed x19, waiting for transfers between devices  194 us
    all_gather x4, waiting for transfers between devices, gather_full(): return lax.all_gather(column, 'rep', axis=0, tiled=False)  76.6 us
    unnamed x144, local copies, waits for them, and re-layouts  66.8 us
    ppermute x16, waiting for transfers between devices, gather_full(): lower.append(lax.ppermute(lower[-1] if lower else piece, 'shard', pairs))  63.7 us
    reduce_scatter x2, waiting for transfers between devices, reduce_full(): part = lax.psum_scatter(part, 'shard', scatter_dimension=0, tiled=True)  50.9 us
    ppermute x12, starting transfers between devices, gather_full(): upper.append(lax.ppermute(upper[-1] if upper else piece, 'shard', back))  43.7 us
    all_gather x3, blocking collectives, reduce_full(): pieces = lax.all_gather(part, 'rep', axis=0, tiled=False)  35.7 us
    dot_general x1, matrix products, attend_backward(): jnp.einsum('hqk,khd->qhd', score_grad, rotated_keys, preferred_element_ty...  26.2 us
  transfers between devices with their start and end apart: 41, of which 31 were waited for; matrix products, arithmetic and copies ran while one was open for 35% of the time, Pallas kernels for 0%

profile of v1, /device:TPU:0, one launch (start us, length us, event | category | flops | bytes accessed | tf_op | source)
XLA Modules:
  0.0 860.8 jit_solution(6162557414397154486)
XLA Ops:
  34.5 7.2 collective-permute-done
  69.9 8.8 %collective-permute-done.14 = bf16[128,1408]{1,0:T(8,128)(2,1)S(1)} collective-permute-done((bf16[128,1408]{1,0:T(8,128)(2,1)S(1)}, bf16[128,1408]{1,0:T(8,128)(2,1)S(1)}, u32[]{:S(2)}, u32[]{:S(2)}) %collective-permute-start.14) | collective-permute-done | bytes 360480 | tf_op jit(solution)/shard_map/ppermute | solution.py:119
  121.1 6.8 collective-permute-done.22
  155.9 8.6 %copy.182 = bf16[4,768,1024]{2,1,0:T(8,128)(2,1)} copy(bf16[4,768,1024]{1,2,0:T(8,128)(2,1)} %bitcast.326) | data formatting | bytes 12582912 | tf_op jit(solution)/shard_map/rd,qde->rqe/dot_general | solution.py:182
  187.6 7.5 fusion.101
  195.1 10.1 %fusion.4 = f32[16,512]{1,0:T(8,128)S(1)} fusion(f32[16,512,512]{1,2,0:T(8,128)} %get-tuple-element.181, f32[16,512]{1,0:T(8,128)S(1)} %get-tuple-element.180), kind=kLoop, calls=%fused_computation.12 | loop fusion | flops 8380416 | bytes 16842752 | tf_op jit(solution)/shard_map/while/body/eval_jaxpr/reduce_sum | solution.py:63
  205.3 7.9 fusion.60
  216.3 43.6 %all-gather.14.cloned.1.call-done = bf16[4,1024,1408]{2,1,0:T(8,128)(2,1)} async-done(((bf16[1,1024,1408]{2,1,0:T(8,128)(2,1)}), bf16[4,1024,1408]{2,1,0:T(8,128)(2,1)}) %all-gather.14.cloned.1.call-update) | async-done | bytes 11534352 | tf_op jit(solution)/shard_map/all_gather | solution.py:126
  259.8 12.6 %fusion.79 = f32[512,4,1408]{0,2,1:T(8,128)} fusion(bf16[4,1024,1408]{2,1,0:T(8,128)(2,1)} %all-gather.14.cloned.1.call-done, f32[512,1024]{1,0:T(8,128)} %copy-done.8, f32[512]{0:T(512)S(1)} %add_rsqrt_fusion, f32[512]{0:T(512)S(1)} %broadcast_multiply_fusion.4), kind=kOutput, calls=%fused_computation.170 | convolution fusion | flops 5907152896 | bytes 25169920 | tf_op jit(solution)/shard_map/rd,qdf->rqf/dot_general | solution.py:199
  272.5 9.9 %fusion.99 = (f32[512,1,2816]{0,2,1:T(8,128)}, f32[512,1,2816]{0,2,1:T(8,128)}) fusion(f32[512,2,2816]{0,2,1:T(8,128)} %bitcast.319), kind=kLoop, calls=%fused_computation.200 | loop fusion | bytes 23068672 | tf_op jit(solution)/shard_map/slice | solution.py:202
  282.4 6.3 copy.240
  294.9 33.0 %all-gather.16.cloned.1.call-done = bf16[4,2816,256]{2,1,0:T(8,128)(2,1)} async-done(((bf16[1,2816,256]{2,1,0:T(8,128)(2,1)}), bf16[4,2816,256]{2,1,0:T(8,128)(2,1)}) %all-gather.16.cloned.1.call-update) | async-done | bytes 5767184 | tf_op jit(solution)/shard_map/all_gather | solution.py:126
  327.9 11.1 %fusion.25 = (bf16[512,2816]{1,0:T(8,128)(2,1)S(1)}, bf16[512,2816]{1,0:T(8,128)(2,1)S(1)}) fusion(f32[512,1,2816]{2,0,1:T(8,128)} %copy.239, f32[512,1,2816]{2,0,1:T(8,128)} %copy.240, bf16[4,2816,256]{2,1,0:T(8,128)(2,1)} %all-gather.16.cloned.1.call-done, f32[512,4,256]{2,1,0:T(4,128)} %reshape.445, f32[512]{0:T(512)S(1)} %fusion.89), kind=kOutput, calls=%fused_computation.34 | convolution fusion | flops 2972581888 | bytes 25167872 | tf_op jit(solution)/shard_map/rqe,qfe->rf/dot_general | solution.py:212
  343.4 11.1 %bitcast_reduce_fusion.1 = (f32[512]{0:T(512)S(1)}, f32[512]{0:T(512)S(1)}, f32[512,1024,1]{1,0,2:T(8,128)S(1)}) fusion(f32[512]{0:T(512)S(1)} %add_rsqrt_fusion, f32[512,1024]{1,0:T(8,128)S(1)} %copy-done.9, f32[512]{0:T(512)S(1)} %broadcast_multiply_fusion.4, bf16[512,4,1408]{2,0,1:T(8,128)(2,1)} %bitcast_dynamic-update-slice_fusion, ...), kind=kOutput, calls=%fused_computation.85 | convolution fusion | flops 5908200448 | bytes 21504000 | tf_op jit(solution)/shard_map/rqf,qdf->rd/dot_general | solution.py:225
  362.2 12.1 %fusion.6 = bf16[4,1024,1408]{1,2,0:T(8,128)(2,1)} fusion(bf16[512,4,1408]{2,0,1:T(8,128)(2,1)} %bitcast_dynamic-update-slice_fusion, f32[512,1024]{1,0:T(8,128)} %copy-done.8, f32[512]{0:T(512)S(1)} %add_rsqrt_fusion, f32[512]{0:T(512)S(1)} %broadcast_multiply_fusion.4), kind=kOutput, calls=%fused_computation.15 | convolution fusion | flops 5912920064 | bytes 19402752 | tf_op jit(solution)/shard_map/rc,rqf->qcf/dot_general | solution.py:238
  375.2 6.3 multiply_convert_fusion.1
  395.2 8.2 fusion.103
  403.4 26.2 %fusion.16 = f32[16,64,512]{2,1,0:T(8,128)} fusion(bf16[512,16,64]{0,2,1:T(8,128)(2,1)} %copy-done.23, f32[16,512,512]{1,2,0:T(8,128)} %fusion.103, f32[16,512,512]{1,2,0:T(8,128)} %get-tuple-element.181, f32[16,512]{1,0:T(8,128)S(1)} %log_add_fusion), kind=kOutput, calls=%fused_computation.23 | convolution fusion | flops 566239744 | bytes 36732928 | tf_op jit(solution)/shard_map/while/body/eval_jaxpr/hqk,khd->qhd/dot_general | solution.py:89
  433.2 26.1 %fusion.13 = f32[16,64,512]{2,1,0:T(8,128)} fusion(bf16[512,16,64]{0,2,1:T(8,128)(2,1)S(1)} %copy-done.22, f32[16,512,512]{1,2,0:T(8,128)} %fusion.103, f32[16,512,512]{1,2,0:T(8,128)} %get-tuple-element.181, f32[16,512]{1,0:T(8,128)S(1)} %log_add_fusion), kind=kOutput, calls=%fused_computation.22 | convolution fusion | flops 566239744 | bytes 36732928 | tf_op jit(solution)/shard_map/while/body/eval_jaxpr/hqk,qhd->khd/dot_general | solution.py:92
  465.1 8.6 fusion.7
  483.7 29.3 %reduce-scatter.37.cloned.1.call-done = bf16[1,1024,1408]{1,2,0:T(8,128)(2,1)} async-done(((bf16[4,1024,1408]{1,2,0:T(8,128)(2,1)}), bf16[1,1024,1408]{1,2,0:T(8,128)(2,1)}) %reduce-scatter.37.cloned.1.call-update) | async-done | bytes 2883600
  517.6 64.5 %reduce-scatter.39.cloned.1.call-done = bf16[1,2816,256]{1,2,0:T(8,128)(2,1)} async-done(((bf16[4,2816,256]{1,2,0:T(8,128)(2,1)}), bf16[1,2816,256]{1,2,0:T(8,128)(2,1)}) %reduce-scatter.39.cloned.1.call-update) | async-done | bytes 1441808
  584.7 70.9 %reduce-scatter.33.cloned.1.call-done = bf16[1,1024,768]{1,2,0:T(8,128)(2,1)} async-done(((bf16[4,1024,768]{1,2,0:T(8,128)(2,1)}), bf16[1,1024,768]{1,2,0:T(8,128)(2,1)}) %reduce-scatter.33.cloned.1.call-update) | async-done | bytes 1572880
  665.6 8.4 copy.193
  674.0 7.2 bitcast_reduce_fusion
  690.4 9.4 %all-gather.1 = bf16[512,256]{0,1:T(8,128)(2,1)S(1)} all-gather(bf16[128,256]{0,1:T(8,128)(2,1)S(1)} %copy.234), channel_id=3, replica_groups=mesh['rep'=4,'shard'=8] {'rep'}, dimensions={0}, use_global_device_ids=true | all-gather | bytes 327680 | tf_op jit(solution)/shard_map/all_gather | solution.py:132
  700.4 28.8 %reduce-scatter.29.cloned.1.call-done = bf16[128,1408]{1,0:T(8,128)(2,1)} async-done(((bf16[1024,1408]{1,0:T(8,128)(2,1)}), bf16[128,1408]{1,0:T(8,128)(2,1)}) %reduce-scatter.29.cloned.1.call-update) | async-done | bytes 360464
  732.5 32.7 %reduce-scatter.31.cloned.1.call-done = bf16[352,256]{1,0:T(8,128)(2,1)} async-done(((bf16[2816,256]{1,0:T(8,128)(2,1)}), bf16[352,256]{1,0:T(8,128)(2,1)}) %reduce-scatter.31.cloned.1.call-update) | async-done | bytes 180240 | tf_op jit(solution)/shard_map/reduce_scatter | solution.py:131
  765.2 11.4 %all-gather.3 = bf16[1408,256]{1,0:T(8,128)(2,1)S(1)} all-gather(bf16[352,256]{1,0:T(8,128)(2,1)} %reduce-scatter.31.cloned.1.call-done), channel_id=5, replica_groups=mesh['rep'=4,'shard'=8] {'rep'}, dimensions={0}, use_global_device_ids=true | all-gather | bytes 901120 | tf_op jit(solution)/shard_map/all_gather | solution.py:132
  782.3 18.2 %reduce-scatter.25.cloned.1.call-done = bf16[128,768]{1,0:T(8,128)(2,1)} async-done(((bf16[1024,768]{1,0:T(8,128)(2,1)}), bf16[128,768]{1,0:T(8,128)(2,1)}) %reduce-scatter.25.cloned.1.call-update) | async-done | bytes 196624 | tf_op jit(solution)/shard_map/reduce_scatter | solution.py:131
  800.5 14.9 %all-gather = bf16[512,768]{1,0:T(8,128)(2,1)S(1)} all-gather(bf16[128,768]{1,0:T(8,128)(2,1)} %reduce-scatter.25.cloned.1.call-done), channel_id=2, replica_groups=mesh['rep'=4,'shard'=8] {'rep'}, dimensions={0}, use_global_device_ids=true | all-gather | bytes 983040 | tf_op jit(solution)/shard_map/all_gather | solution.py:132
  841.8 12.2 %multiply_subtract_fusion = (f32[128,2,2816]{2,1,0:T(2,128)}, f32[128,2,2816]{2,1,0:T(2,128)}, f32[128,2,2816]{2,1,0:T(2,128)}) fusion(f32[128,2,2816]{2,1,0:T(2,128)S(1)} %copy-done.4, f32[]{:T(128)} %bitcast.94, f32[]{:T(128)} %bitcast.93, f32[]{:T(128)} %bitcast.311, f32[128,2,2816]{2,1,0:T(2,128)} %reshape.453, f32[128,2,2816]{2,1,0:T(2,128)} %param.32, ...), kind=kLoop, calls=%fused_computation.49 | loop fusion | flops 10813440 | bytes 20185100 | tf_op jit(solution)/shard_map/sub | solution.py:102
  (302 shorter events, 263.7 us)
Async XLA Ops:
  7.2 144.5 %all-gather.12.cloned.1.call-start = ((), (), s32[]{:S(2)}) async-start(), calls=%async_computation.9 | async-start | bytes 2621440 | tf_op jit(solution)/shard_map/all_gather | solution.py:126
  33.8 122.2 %all-gather.10.cloned.1.call-start = ((), (), s32[]{:S(2)}) async-start(), calls=%async_computation.8 | async-start | bytes 7864320 | tf_op jit(solution)/shard_map/all_gather | solution.py:126
  34.4 7.3 collective-permute-start
  41.7 7.1 collective-permute-start.1
  41.7 7.1 collective-permute-start.4
  48.8 7.1 collective-permute-start.2
  48.8 7.1 collective-permute-start.5
  55.8 6.9 collective-permute-start.3
  55.8 8.1 collective-permute-start.6
  68.6 191.3 %all-gather.14.cloned.1.call-start = ((), (), s32[]{:S(2)}) async-start(), calls=%async_computation.10 | async-start | bytes 14417920 | tf_op jit(solution)/shard_map/all_gather | solution.py:126
  69.8 8.9 %collective-permute-start.14 = (bf16[128,1408]{1,0:T(8,128)(2,1)S(1)}, bf16[128,1408]{1,0:T(8,128)(2,1)S(1)}, u32[]{:S(2)}, u32[]{:S(2)}) collective-permute-start(bf16[128,1408]{1,0:T(8,128)(2,1)S(1)} %constant_dynamic-slice_fusion), channel_id=1, source_target_pairs={{0,1},{1,2},{2,3},{3,4},{4,5},{5,6},{6,7},{7,0},{8,9},{9,10},{10,1... | collective-permute-start | bytes 1081352 | tf_op jit(solution)/shard_map/ppermute | solution.py:119
  78.7 9.0 %collective-permute-start.15 = (bf16[128,1408]{1,0:T(8,128)(2,1)S(1)}, bf16[128,1408]{1,0:T(8,128)(2,1)S(1)}, u32[]{:S(2)}, u32[]{:S(2)}) collective-permute-start(bf16[128,1408]{1,0:T(8,128)(2,1)S(1)} %collective-permute-done.14), channel_id=1, source_target_pairs={{0,1},{1,2},{2,3},{3,4},{4,5},{5,6},{6,7},{7,0},{8,9},{9,10},{10,1... | collective-permute-start | bytes 1081352 | tf_op jit(solution)/shard_map/ppermute | solution.py:119
  78.7 9.8 %collective-permute-start.18 = (bf16[128,1408]{1,0:T(8,128)(2,1)S(1)}, bf16[128,1408]{1,0:T(8,128)(2,1)S(1)}, u32[]{:S(2)}, u32[]{:S(2)}) collective-permute-start(bf16[128,1408]{1,0:T(8,128)(2,1)S(1)} %constant_dynamic-slice_fusion), channel_id=1, source_target_pairs={{1,0},{2,1},{3,2},{4,3},{5,4},{6,5},{7,6},{0,7},{9,8},{10,9},{11,1... | collective-permute-start | bytes 1081352 | tf_op jit(solution)/shard_map/ppermute | solution.py:121
  87.8 8.9 %collective-permute-start.16 = (bf16[128,1408]{1,0:T(8,128)(2,1)S(1)}, bf16[128,1408]{1,0:T(8,128)(2,1)S(1)}, u32[]{:S(2)}, u32[]{:S(2)}) collective-permute-start(bf16[128,1408]{1,0:T(8,128)(2,1)S(1)} %collective-permute-done.15), channel_id=1, source_target_pairs={{0,1},{1,2},{2,3},{3,4},{4,5},{5,6},{6,7},{7,0},{8,9},{9,10},{10,1... | collective-permute-start | bytes 1081352 | tf_op jit(solution)/shard_map/ppermute | solution.py:119
  88.6 9.0 %collective-permute-start.19 = (bf16[128,1408]{1,0:T(8,128)(2,1)S(1)}, bf16[128,1408]{1,0:T(8,128)(2,1)S(1)}, u32[]{:S(2)}, u32[]{:S(2)}) collective-permute-start(bf16[128,1408]{1,0:T(8,128)(2,1)S(1)} %collective-permute-done.18), channel_id=1, source_target_pairs={{1,0},{2,1},{3,2},{4,3},{5,4},{6,5},{7,6},{0,7},{9,8},{10,9},{11,1... | collective-permute-start | bytes 1081352 | tf_op jit(solution)/shard_map/ppermute | solution.py:121
  96.7 8.8 %collective-permute-start.17 = (bf16[128,1408]{1,0:T(8,128)(2,1)S(1)}, bf16[128,1408]{1,0:T(8,128)(2,1)S(1)}, u32[]{:S(2)}, u32[]{:S(2)}) collective-permute-start(bf16[128,1408]{1,0:T(8,128)(2,1)S(1)} %collective-permute-done.16), channel_id=1, source_target_pairs={{0,1},{1,2},{2,3},{3,4},{4,5},{5,6},{6,7},{7,0},{8,9},{9,10},{10,1... | collective-permute-start | bytes 1081352 | tf_op jit(solution)/shard_map/ppermute | solution.py:119
  97.6 10.0 %collective-permute-start.20 = (bf16[128,1408]{1,0:T(8,128)(2,1)S(1)}, bf16[128,1408]{1,0:T(8,128)(2,1)S(1)}, u32[]{:S(2)}, u32[]{:S(2)}) collective-permute-start(bf16[128,1408]{1,0:T(8,128)(2,1)S(1)} %collective-permute-done.19), channel_id=1, source_target_pairs={{1,0},{2,1},{3,2},{4,3},{5,4},{6,5},{7,6},{0,7},{9,8},{10,9},{11,1... | collective-permute-start | bytes 1081352 | tf_op jit(solution)/shard_map/ppermute | solution.py:121
  110.1 217.9 %all-gather.16.cloned.1.call-start = ((), (), s32[]{:S(2)}) async-start(), calls=%async_computation.11 | async-start | bytes 7208960 | tf_op jit(solution)/shard_map/all_gather | solution.py:126
  111.3 9.8 %collective-permute-start.21 = (bf16[352,256]{1,0:T(8,128)(2,1)S(1)}, bf16[352,256]{1,0:T(8,128)(2,1)S(1)}, u32[]{:S(2)}, u32[]{:S(2)}) collective-permute-start(bf16[352,256]{1,0:T(8,128)(2,1)S(1)} %dynamic-slice_convert_fusion), channel_id=1, source_target_pairs={{0,1},{1,2},{2,3},{3,4},{4,5},{5,6},{6,7},{7,0},{8,9},{9,10},{10,1... | collective-permute-start | bytes 540680 | tf_op jit(solution)/shard_map/ppermute | solution.py:119
  111.3 17.0 %collective-permute-start.25 = (bf16[352,256]{1,0:T(8,128)(2,1)S(1)}, bf16[352,256]{1,0:T(8,128)(2,1)S(1)}, u32[]{:S(2)}, u32[]{:S(2)}) collective-permute-start(bf16[352,256]{1,0:T(8,128)(2,1)S(1)} %dynamic-slice_convert_fusion), channel_id=1, source_target_pairs={{1,0},{2,1},{3,2},{4,3},{5,4},{6,5},{7,6},{0,7},{9,8},{10,9},{11,1... | collective-permute-start | bytes 540680 | tf_op jit(solution)/shard_map/ppermute | solution.py:121
  121.0 6.9 collective-permute-start.22
  128.0 6.9 collective-permute-start.23
  135.0 12.3 %collective-permute-start.27 = (bf16[352,256]{1,0:T(8,128)(2,1)S(1)}, bf16[352,256]{1,0:T(8,128)(2,1)S(1)}, u32[]{:S(2)}, u32[]{:S(2)}) collective-permute-start(bf16[352,256]{1,0:T(8,128)(2,1)S(1)} %collective-permute-done.26), channel_id=1, source_target_pairs={{1,0},{2,1},{3,2},{4,3},{5,4},{6,5},{7,6},{0,7},{9,8},{10,9},{11,1... | collective-permute-start | bytes 540680 | tf_op jit(solution)/shard_map/ppermute | solution.py:121
  151.1 330.4 %reduce-scatter.35.cloned.1.call-start = ((), (), s32[]{:S(2)}) async-start(), calls=%async_computation.18 | async-start | bytes 2621440
  362.2 150.8 %reduce-scatter.37.cloned.1.call-start = ((), (), s32[]{:S(2)}) async-start(), calls=%async_computation.19 | async-start | bytes 14417920
  374.4 207.7 %reduce-scatter.39.cloned.1.call-start = ((), (), s32[]{:S(2)}) async-start(), calls=%async_computation.20 | async-start | bytes 7208960
  388.1 267.5 %reduce-scatter.33.cloned.1.call-start = ((), (), s32[]{:S(2)}) async-start(), calls=%async_computation.17 | async-start | bytes 7864320
  481.3 208.1 %reduce-scatter.27.cloned.1.call-start = ((), (), s32[]{:S(2)}) async-start(), calls=%async_computation.14 | async-start | bytes 589824
  483.6 245.5 %reduce-scatter.29.cloned.1.call-start = ((), (), s32[]{:S(2)}) async-start(), calls=%async_computation.15 | async-start | bytes 3244032
  517.5 247.7 %reduce-scatter.31.cloned.1.call-start = ((), (), s32[]{:S(2)}) async-start(), calls=%async_computation.16 | async-start | bytes 1622016 | tf_op jit(solution)/shard_map/reduce_scatter | solution.py:131
  584.6 215.8 %reduce-scatter.25.cloned.1.call-start = ((), (), s32[]{:S(2)}) async-start(), calls=%async_computation.13 | async-start | bytes 1769472 | tf_op jit(solution)/shard_map/reduce_scatter | solution.py:131
  658.1 172.4 %all-gather.18.cloned.1.call-start = ((), (), s32[]{:S(2)}) async-start(), calls=%async_computation.12 | async-start | bytes 1802240 | tf_op jit(solution)/shard_map/all_gather | solution.py:132
  (58 other events, 574.3 us)
Sparse Core Ops, SparseCore 0:
  33.9 37.0 all-gather.11
  73.4 70.1 all-gather.9
  146.0 113.7 all-gather.13
  262.1 65.7 all-gather.15
  362.3 35.1 reduce-scatter.34
  400.8 112.1 reduce-scatter.36
  516.2 65.8 reduce-scatter.38
  585.3 70.1 reduce-scatter.32
  658.5 30.9 reduce-scatter.26
  692.2 36.9 reduce-scatter.28
  732.0 33.1 reduce-scatter.30
  767.9 32.4 reduce-scatter.24
  802.9 27.6 all-gather.17
